TPU v7x, 32 devices: a whole 2x2x4 slice. The times are simulated.
32 devices in a mesh: shard: 2 (over y), ctx: 4 (over x, core), tensor: 4 (over z).
Axes of the slice: x: 2, y: 2, z: 4, core: 2. Of those that a mesh axis runs over, the one named last changes fastest.
Arguments:
- inputs: bfloat16 [2, 1024, 2048], P('shard', 'ctx'), may hold values from -6 to 6
- cotangent: bfloat16 [2, 1024, 2048], P('shard', 'ctx'), may hold values from -6 to 6
- piece_starts: int32 [2, 3], P('shard'), may hold values from 0 to 768, as said below
- positions: int32 [2, 1024], P('shard', 'ctx'), may hold values from 0 to 303, as said below
- w_qkv: float32 [2048, 8, 768], P(('shard', 'ctx'), 'tensor'), may hold values from -0.125 to 0.125
- b_qkv: float32 [8, 768], P('tensor'), may hold values from -1.2 to 1.2
- w_dense: float32 [2048, 8, 256], P(('shard', 'ctx'), 'tensor'), may hold values from -0.5 to 0.5
- w_fc1: float32 [2048, 8192], P(('shard', 'ctx'), 'tensor'), may hold values from -0.125 to 0.125
- b_fc1: float32 [8192], P('tensor'), may hold values from -3 to 3
- w_fc2: float32 [2048, 8192], P(('shard', 'ctx'), 'tensor'), may hold values from -0.0625 to 0.0625
- out_bias: float32 [2048], replicated, may hold values from -3 to 3
- ln1_gain: float32 [2048], replicated, may hold values from 0.1 to 1.9
- ln1_bias: float32 [2048], replicated, may hold values from -2 to 2
- ln2_gain: float32 [2048], replicated, may hold values from 0.1 to 1.9
- ln2_bias: float32 [2048], replicated, may hold values from -2 to 2
Outputs:
- output: bfloat16 [2, 1024, 2048], P('shard', 'ctx')
- grad_inputs: float32 [2, 1024, 2048], P('shard', 'ctx')
- grad_w_qkv: float32 [2048, 8, 768], P(('shard', 'ctx'), 'tensor')
- grad_b_qkv: float32 [8, 768], P('tensor')
- grad_w_dense: float32 [2048, 8, 256], P(('shard', 'ctx'), 'tensor')
- grad_w_fc1: float32 [2048, 8192], P(('shard', 'ctx'), 'tensor')
- grad_b_fc1: float32 [8192], P('tensor')
- grad_w_fc2: float32 [2048, 8192], P(('shard', 'ctx'), 'tensor')
- grad_out_bias: float32 [2048], replicated
- grad_ln1_gain: float32 [2048], replicated
- grad_ln1_bias: float32 [2048], replicated
- grad_ln2_gain: float32 [2048], replicated
- grad_ln2_bias: float32 [2048], replicated
Inputs may be any that keep to these rules, and one draw needn't show every extreme that they name: `piece_starts`: for each sequence, 3 starts in increasing order; its picture pieces of 256 tokens do not intersect and lie inside the sequence. `positions`: in each sequence the position starts at 0 and rises by one at every token outside the picture pieces and at the first of every 16 tokens of a piece; the other tokens of a piece keep the position before them.
All inputs are finite; a program needn't handle non-finite values.
Results may differ from a plain program's by a relative error of at most 0.012.
Values may be sent and summed in bfloat16 or wider, within the bound.
No kernel may reach another device: no remote copies, remote signals or barrier semaphores. Data moves between devices by JAX's collectives and lax.ppermute only.
A program may use at most 256 MiB of HBM per device.

v0:
```python
import jax
import jax.numpy as jnp
from jax import lax
from jax.sharding import PartitionSpec as P

HEAD = 256
ROT = 64
PIECE = 256
PIECES = 3
EPSILON = 1e-05
ROPE_BASE = 10000.0


def layer_norm(values, norm_gain, norm_shift):
    centred = values - jnp.mean(values, axis=-1, keepdims=True)
    spread = jnp.mean(centred * centred, axis=-1, keepdims=True)
    return centred * lax.rsqrt(spread + EPSILON) * norm_gain + norm_shift


def rotary_tables(places):
    half_rot = ROT // 2
    frequency = ROPE_BASE ** (-(jnp.arange(half_rot, dtype=jnp.float32) * 2.0) / ROT)
    angles = places.astype(jnp.float32)[..., None] * frequency
    angles = jnp.concatenate([angles, angles], axis=-1)
    return (jnp.cos(angles)[..., None, :], jnp.sin(angles)[..., None, :])


def rotate(head_values, cosine, sine_part):
    half_rot = ROT // 2
    rotated_part = head_values[..., :ROT]
    turned = jnp.concatenate([-rotated_part[..., half_rot:], rotated_part[..., :half_rot]], axis=-1)
    return jnp.concatenate(
        [rotated_part * cosine + turned * sine_part, head_values[..., ROT:]], axis=-1
    )


def piece_map(token_index, starts):
    inside = (token_index[None, :, None] >= starts[:, None, :]) & (
        token_index[None, :, None] < starts[:, None, :] + PIECE
    )
    labels = jnp.arange(1, PIECES + 1, dtype=jnp.int32)
    return jnp.sum(jnp.where(inside, labels, 0), axis=2)


def exact_gelu(pre_act):
    return jax.nn.gelu(pre_act, approximate=False)


def cross_rows(left_rows, right_rows):
    return lax.dot_general(
        left_rows, right_rows, (((1,), (1,)), ((), ())), preferred_element_type=jnp.float32
    )


def outer_rows(left_rows, right_rows):
    return lax.dot_general(
        left_rows, right_rows, (((0,), (0,)), ((), ())), preferred_element_type=jnp.float32
    )


def local(
    inputs,
    cotangent,
    piece_starts,
    positions,
    w_qkv,
    b_qkv,
    w_dense,
    w_fc1,
    b_fc1,
    w_fc2,
    out_bias,
    ln1_gain,
    ln1_bias,
    ln2_gain,
    ln2_bias,
):
    groups, seq_span, model_width = inputs.shape
    row_count = groups * seq_span
    local_heads = w_qkv.shape[1]
    shard_rows = w_qkv.shape[0]
    seq_length = seq_span * lax.axis_size("ctx")
    score_scale = HEAD ** (-0.5)
    attn_cols = local_heads * HEAD
    joint_cols = local_heads * 3 * HEAD
    residual = inputs.astype(jnp.float32).reshape(row_count, model_width)
    normed_one = layer_norm(residual, ln1_gain, ln1_bias).astype(jnp.bfloat16)
    normed_two = layer_norm(residual, ln2_gain, ln2_bias).astype(jnp.bfloat16)
    qkv_low = w_qkv.astype(jnp.bfloat16)
    dense_low = w_dense.astype(jnp.bfloat16)
    fc1_low = w_fc1.astype(jnp.bfloat16)
    fc2_low = w_fc2.astype(jnp.bfloat16)
    front_qkv, front_fc1 = (
        lax.all_gather(qkv_low, ("shard", "ctx"), axis=0, tiled=True),
        lax.all_gather(fc1_low, ("shard", "ctx"), axis=0, tiled=True),
    )
    joined = jnp.dot(
        normed_one, front_qkv.reshape(model_width, joint_cols), preferred_element_type=jnp.float32
    )
    inner_sum = jnp.dot(normed_two, front_fc1, preferred_element_type=jnp.float32)
    joined = joined.reshape(groups, seq_span, local_heads, 3 * HEAD) + b_qkv
    cosine, sine_part = rotary_tables(positions)
    queries = rotate(joined[..., :HEAD], cosine, sine_part).astype(jnp.bfloat16)
    key_rows = rotate(joined[..., HEAD : 2 * HEAD], cosine, sine_part).astype(jnp.bfloat16)
    value_rows = joined[..., 2 * HEAD :].astype(jnp.bfloat16)
    all_keys, all_values = (
        lax.all_gather(key_rows, "ctx", axis=1, tiled=True),
        lax.all_gather(value_rows, "ctx", axis=1, tiled=True),
    )
    key_index = jnp.arange(seq_length, dtype=jnp.int32)
    query_index = lax.axis_index("ctx") * seq_span + jnp.arange(seq_span, dtype=jnp.int32)
    key_piece = piece_map(key_index, piece_starts)
    query_piece = piece_map(query_index, piece_starts)
    allowed = (key_index[None, None, :] <= query_index[None, :, None]) | (
        key_piece[:, None, :] == query_piece[:, :, None]
    ) & (query_piece[:, :, None] > 0)

    def score_block(query_low):
        raw_scores = (
            jnp.einsum("gqhd,gkhd->ghqk", query_low, all_keys, preferred_element_type=jnp.float32)
            * score_scale
        )
        return jnp.where(allowed[:, None], raw_scores, -1e30)

    scores = score_block(queries)
    row_max = jnp.max(scores, axis=-1, keepdims=True)
    exponent = jnp.exp(scores - row_max)
    row_total = jnp.sum(exponent, axis=-1, keepdims=True)
    weights = exponent / row_total
    log_total = row_max + jnp.log(row_total)
    attended = jnp.einsum(
        "ghqk,gkhd->gqhd",
        weights.astype(jnp.bfloat16),
        all_values,
        preferred_element_type=jnp.float32,
    )
    context = attended.reshape(row_count, attn_cols).astype(jnp.bfloat16)
    pre_gelu = inner_sum + b_fc1
    hidden = exact_gelu(pre_gelu).astype(jnp.bfloat16)
    piece_pair = (
        lax.all_gather(dense_low, ("shard", "ctx"), axis=0, tiled=True),
        lax.all_gather(fc2_low, ("shard", "ctx"), axis=0, tiled=True),
    )
    row_span = piece_pair[0].shape[0]
    block_out = cross_rows(context, piece_pair[0].reshape(row_span, attn_cols)) + cross_rows(
        hidden, piece_pair[1]
    )
    summed_out = lax.psum(block_out, "tensor")
    output = (
        (residual + summed_out + out_bias)
        .astype(jnp.bfloat16)
        .reshape(groups, seq_span, model_width)
    )
    grad_low = cotangent.reshape(row_count, model_width)
    grad_flat = grad_low.astype(jnp.float32)
    back_dense, back_fc2 = (
        lax.all_gather(dense_low, ("shard", "ctx"), axis=0, tiled=True),
        lax.all_gather(fc2_low, ("shard", "ctx"), axis=0, tiled=True),
    )
    grad_context = jnp.dot(
        grad_low, back_dense.reshape(model_width, attn_cols), preferred_element_type=jnp.float32
    )
    grad_hidden = jnp.dot(grad_low, back_fc2, preferred_element_type=jnp.float32)
    outer_sum = lax.psum_scatter(
        jnp.concatenate([outer_rows(grad_low, context), outer_rows(grad_low, hidden)], axis=1),
        ("shard", "ctx"),
        scatter_dimension=0,
        tiled=True,
    )
    grad_w_dense = outer_sum[:, :attn_cols].reshape(shard_rows, local_heads, HEAD)
    grad_w_fc2 = outer_sum[:, attn_cols:]
    gelu_value, gelu_back = jax.vjp(exact_gelu, pre_gelu)
    grad_inner = gelu_back(grad_hidden)[0].astype(jnp.bfloat16)
    grad_mixed = grad_context.astype(jnp.bfloat16).reshape(groups, seq_span, local_heads, HEAD)
    probs_again = jnp.exp(score_block(queries) - log_total)
    grad_probs = jnp.einsum(
        "gqhd,gkhd->ghqk", grad_mixed, all_values, preferred_element_type=jnp.float32
    )
    centre = jnp.sum(probs_again * grad_probs, axis=-1, keepdims=True)
    grad_scores = (probs_again * (grad_probs - centre)).astype(jnp.bfloat16)
    grad_queries = (
        jnp.einsum("ghqk,gkhd->gqhd", grad_scores, all_keys, preferred_element_type=jnp.float32)
        * score_scale
    )
    key_terms = (
        jnp.einsum("ghqk,gqhd->gkhd", grad_scores, queries, preferred_element_type=jnp.float32)
        * score_scale
    )
    value_terms = jnp.einsum(
        "ghqk,gqhd->gkhd",
        probs_again.astype(jnp.bfloat16),
        grad_mixed,
        preferred_element_type=jnp.float32,
    )
    grad_keys, grad_values = (
        lax.psum_scatter(key_terms, "ctx", scatter_dimension=1, tiled=True),
        lax.psum_scatter(value_terms, "ctx", scatter_dimension=1, tiled=True),
    )
    back_query = rotate(grad_queries, cosine, -sine_part)
    back_key = rotate(grad_keys, cosine, -sine_part)
    grad_joined = (
        jnp.concatenate([back_query, back_key, grad_values], axis=-1)
        .reshape(row_count, joint_cols)
        .astype(jnp.bfloat16)
    )
    piece_pair = (
        lax.all_gather(qkv_low, ("shard", "ctx"), axis=0, tiled=True),
        lax.all_gather(fc1_low, ("shard", "ctx"), axis=0, tiled=True),
    )
    row_span = piece_pair[0].shape[0]
    block_one = cross_rows(grad_joined, piece_pair[0].reshape(row_span, joint_cols))
    block_two = cross_rows(grad_inner, piece_pair[1])
    grad_norm_one = block_one
    grad_norm_two = block_two
    inner_grads = lax.psum_scatter(
        jnp.concatenate(
            [outer_rows(normed_one, grad_joined), outer_rows(normed_two, grad_inner)], axis=1
        ),
        ("shard", "ctx"),
        scatter_dimension=0,
        tiled=True,
    )
    grad_w_qkv = inner_grads[:, :joint_cols].reshape(shard_rows, local_heads, 3 * HEAD)
    grad_w_fc1 = inner_grads[:, joint_cols:]
    grad_norm_one, grad_norm_two = lax.psum((grad_norm_one, grad_norm_two), "tensor")
    norm_value_one, norm_back_one = jax.vjp(layer_norm, residual, ln1_gain, ln1_bias)
    norm_value_two, norm_back_two = jax.vjp(layer_norm, residual, ln2_gain, ln2_bias)
    grad_res_one, grad_gain_one, grad_shift_one = norm_back_one(grad_norm_one)
    grad_res_two, grad_gain_two, grad_shift_two = norm_back_two(grad_norm_two)
    grad_inputs = (grad_flat + grad_res_one + grad_res_two).reshape(groups, seq_span, model_width)
    bias_qkv_term = jnp.sum(grad_joined.astype(jnp.float32), axis=0).reshape(local_heads, 3 * HEAD)
    bias_fc1_term = jnp.sum(grad_inner.astype(jnp.float32), axis=0)
    small_sums = lax.psum(
        (
            bias_qkv_term,
            bias_fc1_term,
            jnp.sum(grad_flat, axis=0),
            grad_gain_one,
            grad_shift_one,
            grad_gain_two,
            grad_shift_two,
        ),
        ("shard", "ctx"),
    )
    return (
        output,
        grad_inputs,
        grad_w_qkv,
        small_sums[0],
        grad_w_dense,
        grad_w_fc1,
        small_sums[1],
        grad_w_fc2,
        small_sums[2],
        small_sums[3],
        small_sums[4],
        small_sums[5],
        small_sums[6],
    )


def solution(mesh):
    in_specs = (
        P("shard", "ctx", None),
        P("shard", "ctx", None),
        P("shard", None),
        P("shard", "ctx"),
        P(("shard", "ctx"), "tensor", None),
        P("tensor", None),
        P(("shard", "ctx"), "tensor", None),
        P(("shard", "ctx"), "tensor"),
        P("tensor"),
        P(("shard", "ctx"), "tensor"),
        P(),
        P(),
        P(),
        P(),
        P(),
    )
    out_specs = (
        P("shard", "ctx", None),
        P("shard", "ctx", None),
        P(("shard", "ctx"), "tensor", None),
        P("tensor", None),
        P(("shard", "ctx"), "tensor", None),
        P(("shard", "ctx"), "tensor"),
        P("tensor"),
        P(("shard", "ctx"), "tensor"),
        P(),
        P(),
        P(),
        P(),
        P(),
    )
    return jax.shard_map(local, mesh=mesh, in_specs=in_specs, out_specs=out_specs, check_vma=False)
```

profile of v0, /device:TPU:0, one launch (start us, length us, event | category | flops | bytes accessed | tf_op | source)
XLA Modules:
  0.0 868.9 jit_solution(4241122452107551407)
XLA Ops:
  7.3 2.9 convert_element_type.123
  10.3 0.9 convert_element_type.130
  11.4 1.2 fusion.70
  13.3 45.3 %all-gather.7.cloned.1.call-done = bf16[2048,2,768]{2,1,0:T(2,128)(2,1)} async-done(((bf16[256,2,768]{2,1,0:T(2,128)(2,1)}), bf16[2048,2,768]{2,1,0:T(2,128)(2,1)}) %all-gather.7.cloned.1.call-update) | async-done | bytes 6291472 | tf_op jit(solution)/shard_map/all_gather | solution.py:94
  58.6 6.8 copy.109
  65.4 8.8 %copy.74 = bf16[2048,1536]{0,1:T(8,128)(2,1)} copy(bf16[2048,1536]{1,0:T(8,128)(2,1)} %bitcast.158) | data formatting | bytes 12582912 | tf_op jit(solution)/shard_map/reshape | solution.py:98
  74.2 4.6 fusion.81
  78.9 0.9 slice_bitcast_fusion
  81.8 1.7 slice.103
  83.6 1.1 convert_element_type.132
  84.8 2.7 convert_element_type.134
  87.9 1.1 fusion.53
  88.9 2.1 copy.110
  91.1 1.3 copy-done.4
  93.2 14.6 %all-gather.11.cloned.1.call-done = bf16[1,1024,2,256]{3,1,2,0:T(8,128)(2,1)} async-done(((bf16[1,256,2,256]{3,1,2,0:T(8,128)(2,1)}), bf16[1,1024,2,256]{3,1,2,0:T(8,128)(2,1)}) %all-gather.11.cloned.1.call-update) | async-done | bytes 1048592 | tf_op jit(solution)/shard_map/all_gather | solution.py:107
  107.8 2.0 fusion.82
  110.9 15.6 %all-gather.9.cloned.1.call-done = bf16[1,1024,2,256]{3,1,2,0:T(8,128)(2,1)} async-done(((bf16[1,256,2,256]{3,1,2,0:T(8,128)(2,1)}), bf16[1,1024,2,256]{3,1,2,0:T(8,128)(2,1)}) %all-gather.9.cloned.1.call-update) | async-done | bytes 1048592 | tf_op jit(solution)/shard_map/all_gather | solution.py:108
  126.5 1.7 multiply_reduce_fusion
  128.8 1.0 copy-done.3
  129.8 1.9 multiply_bitcast_fusion
  131.9 2.1 fusion.34
  135.6 1.8 copy.90
  137.4 1.9 convolution_bitcast_fusion.2
  139.3 1.9 slice_negate_fusion.1
  141.3 2.0 convolution_convert_fusion
  143.3 39.8 %all-gather.15.cloned.1.call-done = bf16[2048,2048]{1,0:T(8,128)(2,1)} async-done(((bf16[256,2048]{1,0:T(8,128)(2,1)}), bf16[2048,2048]{1,0:T(8,128)(2,1)}) %all-gather.15.cloned.1.call-update) | async-done | bytes 8388624 | tf_op jit(solution)/shard_map/all_gather | solution.py:95
  183.1 7.1 convolution_add_fusion.1
  190.2 49.5 %all-gather.17.cloned.1.call-done = bf16[2048,2048]{1,0:T(8,128)(2,1)} async-done(((bf16[256,2048]{1,0:T(8,128)(2,1)}), bf16[2048,2048]{1,0:T(8,128)(2,1)}) %all-gather.17.cloned.1.call-update) | async-done | bytes 8388624 | tf_op jit(solution)/shard_map/all_gather | solution.py:142
  239.7 10.6 %fusion.78 = f32[256,2048]{1,0:T(8,128)S(1)} fusion(bf16[2048,2048]{1,0:T(8,128)(2,1)} %all-gather.17.cloned.1.call-done, f32[256,2048]{1,0:T(8,128)} %convolution_add_fusion.1), kind=kOutput, calls=%fused_computation.149 | convolution fusion | flops 2181562368 | bytes 12582912 | tf_op jit(solution)/shard_map/dot_general | solution.py:50
  250.4 2.1 convolution_add_fusion
  252.5 8.2 convert_reduce_fusion.2
  260.7 1.0 copy-done.14
  261.7 3.7 fusion.84
  265.3 8.1 reduce-scatter.5.cloned.1.call-done
  273.4 1.3 slice.153
  275.5 1.2 slice_negate_fusion
  276.8 1.8 fusion.55
  278.6 1.0 copy.91
  279.6 1.0 copy.89
  280.6 1.0 constant_dynamic-update-slice_fusion.2
  281.6 0.9 constant_dynamic-update-slice_fusion
  282.6 24.6 %reduce-scatter.7.cloned.1.call-done = f32[1,256,2,256]{1,3,2,0:T(8,128)} async-done(((f32[1,1024,2,256]{1,3,2,0:T(8,128)}), f32[1,256,2,256]{1,3,2,0:T(8,128)}) %reduce-scatter.7.cloned.1.call-update) | async-done | bytes 524304 | tf_op jit(solution)/shard_map/reduce_scatter | solution.py:197
  307.1 1.1 convert_dynamic-update-slice_fusion
  308.2 6.0 fusion.83
  316.2 0.9 copy-done.42
  317.0 6.6 convolution_bitcast_fusion
  323.6 11.0 %pad_maximum_fusion.1 = f32[2048,2560]{0,1:T(8,128)} fusion(f32[2048,2048]{0,1:T(8,128)S(1)} %convolution_bitcast_fusion, f32[2048,512]{0,1:T(8,128)S(1)} %convolution_bitcast_fusion.1), kind=kLoop, calls=%fused_computation.1 | loop fusion | flops 5242880 | bytes 41943040 | tf_op jit(solution)/shard_map/concatenate | solution.py:165
  335.3 3.8 fusion.73
  339.1 2.0 fusion.50
  341.1 12.3 %pad_maximum_fusion = f32[2048,3584]{0,1:T(8,128)} fusion(f32[2048,2048]{0,1:T(8,128)S(1)} %fusion.73, f32[2048,1536]{0,1:T(8,128)S(1)} %fusion.50), kind=kLoop, calls=%fused_computation | loop fusion | flops 7340032 | bytes 58720256 | tf_op jit(solution)/shard_map/concatenate | solution.py:216
  353.7 183.6 %all-reduce.4.cloned.1.call-done = (f32[256,2048]{1,0:T(8,128)}, f32[256,2048]{1,0:T(8,128)}, f32[256,2048]{1,0:T(8,128)}) async-done(((f32[256,2048]{1,0:T(8,128)}, f32[256,2048]{1,0:T(8,128)}, f32[256,2048]{1,0:T(8,128)}), (f32[256,2048]{1,0:T(8,128)}, f32[256,2048]{1,0:T(8,128)}, f32[256,2048]{1,0:T(8,128)})) %all-reduce.4.cloned.1.call-update) | async-done | bytes 6291472 | tf_op jit(solution)/shard_map/psum | solution.py:148
  537.3 3.2 fusion.80
  540.8 1.7 fusion.16
  542.5 3.3 convert_reduce_fusion.1
  545.8 24.9 %all-reduce = (f32[2,768]{1,0:T(2,128)}, f32[2048]{0:T(1024)}, f32[2048]{0:T(1024)}, f32[2048]{0:T(1024)}, f32[2048]{0:T(1024)}, /*index=5*/f32[2048]{0:T(1024)}, f32[2048]{0:T(1024)}) all-reduce(f32[2,768]{1,0:T(2,128)S(1)} %convert_reduce_fusion.3, ...), channel_id=1, replica_groups=mesh['shard'=2,'ctx'=4,'tensor'=4] {'shard','ctx'}, use_global_device_ids=true, to_apply=%region_18.19 | all-reduce | flops 13824 | bytes 110592 | tf_op jit(solution)/shard_map/psum | solution.py:233
  570.7 105.1 %reduce-scatter.11.cloned.1.call-done = f32[256,2560]{0,1:T(8,128)} async-done(((f32[2048,2560]{0,1:T(8,128)}), f32[256,2560]{0,1:T(8,128)}) %reduce-scatter.11.cloned.1.call-update) | async-done | bytes 2621456 | tf_op jit(solution)/shard_map/reduce_scatter | solution.py:164
  675.8 1.6 slice-done
  677.4 1.8 copy.96
  679.2 1.0 copy.94
  680.2 175.1 %reduce-scatter.9.cloned.1.call-done = f32[256,3584]{0,1:T(8,128)} async-done(((f32[2048,3584]{0,1:T(8,128)}), f32[256,3584]{0,1:T(8,128)}) %reduce-scatter.9.cloned.1.call-update) | async-done | bytes 3670032 | tf_op jit(solution)/shard_map/reduce_scatter | solution.py:215
  855.3 1.6 slice-done.2
  856.9 1.8 copy.95
  858.7 1.4 slice-done.3
  860.1 2.1 copy.93
  (145 shorter events, 11.9 us)
Async XLA Ops:
  7.2 3.1 copy-start.20
  7.2 4.0 copy-start.38
  7.2 5.4 copy-start
  7.2 51.4 %all-gather.7.cloned.1.call-start = ((), (), s32[]{:S(2)}) async-start(), calls=%async_computation.4 | async-start | bytes 7077888 | tf_op jit(solution)/shard_map/all_gather | solution.py:94
  10.2 78.7 %all-gather.13.cloned.1.call-start = ((), (), s32[]{:S(2)}) async-start(), calls=%async_computation.7 | async-start | bytes 2359296 | tf_op jit(solution)/shard_map/all_gather | solution.py:141
  11.2 96.6 %all-gather.11.cloned.1.call-start = ((), (), s32[]{:S(2)}) async-start(), calls=%async_computation.6 | async-start | bytes 1310720 | tf_op jit(solution)/shard_map/all_gather | solution.py:107
  12.8 61.3 %copy-start.24 = (f32[256]{0:T(256)}, f32[256]{0:T(256)S(1)}, u32[]{:S(2)}) copy-start(f32[256]{0:T(256)S(1)} %broadcast_multiply_fusion.1) | copy-start | bytes 3076
  13.3 52.1 %copy-start.28 = (f32[256]{0:T(256)}, f32[256]{0:T(256)S(1)}, u32[]{:S(2)}) copy-start(f32[256]{0:T(256)S(1)} %fusion.17) | copy-start | bytes 3076
  13.3 60.9 %copy-start.26 = (f32[256]{0:T(256)}, f32[256]{0:T(256)S(1)}, u32[]{:S(2)}) copy-start(f32[256]{0:T(256)S(1)} %fusion.67) | copy-start | bytes 3076
  65.4 8.8 %copy-start.22 = (f32[2048]{0:T(1024)S(1)}, f32[2048]{0:T(1024)}, u32[]{:S(2)}) copy-start(f32[2048]{0:T(1024)} %param.26) | copy-start | bytes 24580
  65.4 8.8 %copy-start.30 = (f32[2048]{0:T(1024)S(1)}, f32[2048]{0:T(1024)}, u32[]{:S(2)}) copy-start(f32[2048]{0:T(1024)} %param.27) | copy-start | bytes 24580
  65.4 8.8 %copy-start.40 = (f32[2,768]{1,0:T(2,128)S(1)}, f32[2,768]{1,0:T(2,128)}, u32[]{:S(2)}) copy-start(f32[2,768]{1,0:T(2,128)} %param.20) | copy-start | bytes 18436
  78.9 2.0 copy-start.18
  78.9 1.2 copy-start.21
  80.0 3.6 copy-start.11
  81.8 44.7 %all-gather.9.cloned.1.call-start = ((), (), s32[]{:S(2)}) async-start(), calls=%async_computation.5 | async-start | bytes 1310720 | tf_op jit(solution)/shard_map/all_gather | solution.py:108
  83.5 99.6 %all-gather.15.cloned.1.call-start = ((), (), s32[]{:S(2)}) async-start(), calls=%async_computation.8 | async-start | bytes 9437184 | tf_op jit(solution)/shard_map/all_gather | solution.py:95
  84.7 2.9 copy-start.37
  84.7 155.0 %all-gather.17.cloned.1.call-start = ((), (), s32[]{:S(2)}) async-start(), calls=%async_computation.9 | async-start | bytes 9437184 | tf_op jit(solution)/shard_map/all_gather | solution.py:142
  87.6 185.9 %reduce-scatter.5.cloned.1.call-start = ((), (), s32[]{:S(2)}) async-start(), calls=%async_computation.10 | async-start | bytes 2621440 | tf_op jit(solution)/shard_map/reduce_scatter | solution.py:196
  88.9 3.5 copy-start.8
  91.1 1.3 copy-start.4
  109.8 0.6 copy-start.34
  110.4 0.6 copy-start.35
  128.2 1.5 copy-start.15
  128.2 1.5 copy-start.19
  128.8 1.0 copy-start.3
  131.7 175.4 %reduce-scatter.7.cloned.1.call-start = ((), (), s32[]{:S(2)}) async-start(), calls=%async_computation.11 | async-start | bytes 2621440 | tf_op jit(solution)/shard_map/reduce_scatter | solution.py:197
  134.0 0.8 copy-start.6
  141.3 41.9 %copy-start.23 = (f32[2048]{0:T(1024)S(1)}, f32[2048]{0:T(1024)}, u32[]{:S(2)}) copy-start(f32[2048]{0:T(1024)} %param.28) | copy-start | bytes 24580
  141.3 396.0 %all-reduce.4.cloned.1.call-start = ((), (), s32[]{:S(2)}) async-start(), calls=%async_computation.14 | async-start | bytes 12582912 | tf_op jit(solution)/shard_map/psum | solution.py:148
  190.2 60.1 %copy-start.5 = (bf16[256,8,2,256]{3,1,2,0:T(8,128)(2,1)S(1)}, bf16[256,8,2,256]{3,1,2,0:T(8,128)(2,1)}, u32[]{:S(2)}) copy-start(bf16[256,8,2,256]{3,1,2,0:T(8,128)(2,1)} %copy-done.4) | copy-start | bytes 6291460
  239.7 12.7 %copy-start.39 = (bf16[2048,2048]{1,0:T(8,128)(2,1)S(1)}, bf16[2048,2048]{1,0:T(8,128)(2,1)}, u32[]{:S(2)}) copy-start(bf16[2048,2048]{1,0:T(8,128)(2,1)} %all-gather.17.cloned.1.call-done) | copy-start | bytes 25165828
  239.7 12.7 %copy-start.41 = (f32[256,2048]{1,0:T(8,128)S(1)}, f32[256,2048]{1,0:T(8,128)}, u32[]{:S(2)}) copy-start(f32[256,2048]{1,0:T(8,128)} %convolution_add_fusion.1) | copy-start | bytes 6291460
  250.3 2.1 copy-start.9
  250.4 11.3 %slice-start.4 = ((s8[8388608]{0:T(1024)(128)(4,1)}), s8[4194304]{0:T(1024)(128)(4,1)S(1)}, s32[]{:S(2)}) async-start(s8[8388608]{0:T(1024)(128)(4,1)} %bitcast.176), calls=%async_computation.19 | async-start | bytes 8388608
  252.5 9.2 %slice-start.5 = ((s8[8388608]{0:T(1024)(128)(4,1)}), s8[4194304]{0:T(1024)(128)(4,1)S(1)}, s32[]{:S(2)}) async-start(s8[8388608]{0:T(1024)(128)(4,1)} %bitcast.176), calls=%async_computation.20 | async-start | bytes 8388608
  260.7 1.0 copy-start.14
  265.3 11.4 %copy-start.7 = (f32[1,256,2,256]{3,1,2,0:T(8,128)S(1)}, f32[1,256,2,256]{3,1,2,0:T(8,128)}, u32[]{:S(2)}) copy-start(f32[1,256,2,256]{3,1,2,0:T(8,128)} %copy-done.6) | copy-start | bytes 1572868
  265.3 11.4 %copy-start.16 = (f32[1,256,2,32]{3,1,2,0:T(8,128)S(1)}, f32[1,256,2,32]{3,1,2,0:T(8,128)}, u32[]{:S(2)}) copy-start(f32[1,256,2,32]{3,1,2,0:T(8,128)} %get-tuple-element.89) | copy-start | bytes 196612
  265.3 11.4 %copy-start.17 = (f32[1,256,2,32]{3,1,2,0:T(8,128)S(1)}, f32[1,256,2,32]{3,1,2,0:T(8,128)}, u32[]{:S(2)}) copy-start(f32[1,256,2,32]{3,1,2,0:T(8,128)} %get-tuple-element.90) | copy-start | bytes 196612
  273.4 3.3 copy-start.13
  314.2 1.2 copy-start.10
  314.2 361.6 %reduce-scatter.11.cloned.1.call-start = ((), (), s32[]{:S(2)}) async-start(), calls=%async_computation.13 | async-start | bytes 23592960 | tf_op jit(solution)/shard_map/reduce_scatter | solution.py:164
  315.4 1.6 copy-start.42
  334.6 0.7 copy-start.25
  334.6 0.7 copy-start.27
  334.6 0.7 copy-start.32
  334.6 4.5 copy-start.31
  334.7 520.7 %reduce-scatter.9.cloned.1.call-start = ((), (), s32[]{:S(2)}) async-start(), calls=%async_computation.12 | async-start | bytes 33030144 | tf_op jit(solution)/shard_map/reduce_scatter | solution.py:215
  537.3 3.2 copy-start.29
  537.3 3.3 copy-start.1
  537.3 3.5 copy-start.2
  540.8 1.8 copy-start.12
  540.8 1.8 copy-start.36
  542.5 3.3 copy-start.33
  675.8 1.6 slice-start
  677.4 1.8 slice-start.1
  855.3 1.6 slice-start.2
  858.7 1.4 slice-start.3
Sparse Core Ops, SparseCore 0:
  10.5 48.1 all-gather.6
  61.1 27.7 all-gather.12
  91.0 16.6 all-gather.10
  109.8 16.6 all-gather.8
  128.8 54.2 all-gather.14
  185.4 54.2 all-gather.16
  242.2 31.1 reduce-scatter.4
  275.9 31.1 reduce-scatter.6
  314.4 222.8 all-reduce.3
  540.7 135.0 reduce-scatter.10
  679.4 175.8 reduce-scatter.8
where the time goes:
time: 878 us; the launch traced here: 869 us
  waiting for transfers between devices  661 us (75%)
  matrix products  67.6 us (8%)
  other arithmetic  51.4 us (6%)
  local copies, waits for them, and re-layouts  47.7 us (5%)
  blocking collectives  24.9 us (3%)
  between operations  14.7 us (2%)
    psum x1, waiting for transfers between devices, local(): summed_out = lax.psum(block_out, 'tensor')  184 us
    reduce_scatter x1, waiting for transfers between devices, local(): lax.psum_scatter(jnp.concatenate([outer_rows(normed_one, grad_joined), ou...  175 us
    reduce_scatter x1, waiting for transfers between devices, local(): lax.psum_scatter(jnp.concatenate([outer_rows(grad_low, context), outer_ro...  105 us
    all_gather x1, waiting for transfers between devices, local(): lax.all_gather(fc2_low, ('shard', 'ctx'), axis=0, tiled=True)  49.5 us
    all_gather x1, waiting for transfers between devices, local(): lax.all_gather(qkv_low, ('shard', 'ctx'), axis=0, tiled=True)  45.3 us
    all_gather x1, waiting for transfers between devices, local(): lax.all_gather(fc1_low, ('shard', 'ctx'), axis=0, tiled=True)  39.8 us
    unnamed x100, local copies, waits for them, and re-layouts  24.9 us
    psum x1, blocking collectives, local(): lax.psum((bias_qkv_term, bias_fc1_term, jnp.sum(grad_flat, axis=0), grad_...  24.9 us
  transfers between devices with their start and end apart: 11, of which 10 were waited for; matrix products, arithmetic and copies ran while one was open for 16% of the time, Pallas kernels for 0%

commit v1 on v0

--- a/solution.py
+++ b/solution.py
@@ -145,7 +145,7 @@
     block_out = cross_rows(context, piece_pair[0].reshape(row_span, attn_cols)) + cross_rows(
         hidden, piece_pair[1]
     )
-    summed_out = lax.psum(block_out, "tensor")
+    summed_out = jnp.sum(lax.all_gather(block_out, "tensor"), axis=0)
     output = (
         (residual + summed_out + out_bias)
         .astype(jnp.bfloat16)

time: 878 us -> 961 us (1.095)
  waiting for transfers between devices: 661 us -> 731 us
    all_gather x0 -> x1, waiting for transfers between devices: none -> 116 us  [local(): summed_out = jnp.sum(lax.all_gather(block_out, 'tensor'), axis=0)]
    psum x1, waiting for transfers between devices: 184 us -> 101 us  [local(): lax.psum((grad_norm_one, grad_norm_two), 'tensor')]
    reduce_scatter x1, waiting for transfers between devices: 105 us -> 132 us  [local(): lax.psum_scatter(jnp.concatenate([outer_rows(grad_low, context), outer_ro...]
    reduce_scatter x1, waiting for transfers between devices: 8.08 us -> 18.4 us  [local(): lax.psum_scatter(key_terms, 'ctx', scatter_dimension=1, tiled=True)]
    unnamed x100 -> x98, local copies, waits for them, and re-layouts: 24.9 us -> 28.8 us
  transfers between devices with their start and end apart: 11 -> 12, of which waited for: 10 -> 11; matrix products, arithmetic and copies ran while one was open for 16% -> 16% of each run, Pallas kernels for 0% -> 0%
where the time goes in v1:
time: 961 us; the launch traced here: 952 us
  waiting for transfers between devices  731 us (76%)
  matrix products  68.3 us (7%)
  other arithmetic  59 us (6%)
  local copies, waits for them, and re-layouts  51.6 us (5%)
  blocking collectives  26.4 us (3%)
  between operations  15 us (2%)
    reduce_scatter x1, waiting for transfers between devices, local(): lax.psum_scatter(jnp.concatenate([outer_rows(normed_one, grad_joined), ou...  175 us
    reduce_scatter x1, waiting for transfers between devices, local(): lax.psum_scatter(jnp.concatenate([outer_rows(grad_low, context), outer_ro...  132 us
    all_gather x1, waiting for transfers between devices, local(): summed_out = jnp.sum(lax.all_gather(block_out, 'tensor'), axis=0)  116 us
    psum x1, waiting for transfers between devices, local(): lax.psum((grad_norm_one, grad_norm_two), 'tensor')  101 us
    all_gather x1, waiting for transfers between devices, local(): lax.all_gather(fc2_low, ('shard', 'ctx'), axis=0, tiled=True)  49.5 us
    all_gather x1, waiting for transfers between devices, local(): lax.all_gather(qkv_low, ('shard', 'ctx'), axis=0, tiled=True)  45.3 us
    all_gather x1, waiting for transfers between devices, local(): lax.all_gather(fc1_low, ('shard', 'ctx'), axis=0, tiled=True)  41.4 us
    unnamed x98, local copies, waits for them, and re-layouts  28.8 us
  transfers between devices with their start and end apart: 12, of which 11 were waited for; matrix products, arithmetic and copies ran while one was open for 16% of the time, Pallas kernels for 0%

profile of v1, /device:TPU:0, one launch (start us, length us, event | category | flops | bytes accessed | tf_op | source)
XLA Modules:
  0.0 952.3 jit_solution(12917937584237745118)
XLA Ops:
  7.3 2.9 convert_element_type.124
  11.4 1.2 fusion.68
  13.3 45.3 %all-gather.9.cloned.1.call-done = bf16[2048,2,768]{2,1,0:T(2,128)(2,1)} async-done(((bf16[256,2,768]{2,1,0:T(2,128)(2,1)}), bf16[2048,2,768]{2,1,0:T(2,128)(2,1)}) %all-gather.9.cloned.1.call-update) | async-done | bytes 6291472 | tf_op jit(solution)/shard_map/all_gather | solution.py:94
  58.6 6.8 copy.109
  65.4 8.8 copy.74
  74.2 4.6 fusion.79
  81.8 1.7 slice.103
  83.6 1.1 convert_element_type.133
  84.8 2.7 convert_element_type.135
  87.9 1.1 fusion.51
  88.9 2.1 copy.110
  91.1 1.3 copy-done.4
  93.2 14.6 %all-gather.13.cloned.1.call-done = bf16[1,1024,2,256]{3,1,2,0:T(8,128)(2,1)} async-done(((bf16[1,256,2,256]{3,1,2,0:T(8,128)(2,1)}), bf16[1,1024,2,256]{3,1,2,0:T(8,128)(2,1)}) %all-gather.13.cloned.1.call-update) | async-done | bytes 1048592 | tf_op jit(solution)/shard_map/all_gather | solution.py:107
  107.8 2.0 fusion.80
  111.0 15.6 %all-gather.11.cloned.1.call-done = bf16[1,1024,2,256]{3,1,2,0:T(8,128)(2,1)} async-done(((bf16[1,256,2,256]{3,1,2,0:T(8,128)(2,1)}), bf16[1,1024,2,256]{3,1,2,0:T(8,128)(2,1)}) %all-gather.11.cloned.1.call-update) | async-done | bytes 1048592 | tf_op jit(solution)/shard_map/all_gather | solution.py:108
  126.5 1.7 multiply_reduce_fusion
  129.8 1.9 multiply_bitcast_fusion
  132.3 2.1 fusion.33
  136.0 1.8 copy.90
  137.8 1.9 convolution_bitcast_fusion.2
  139.7 2.0 slice_negate_fusion.1
  141.8 41.4 %all-gather.17.cloned.1.call-done = bf16[2048,2048]{1,0:T(8,128)(2,1)} async-done(((bf16[256,2048]{1,0:T(8,128)(2,1)}), bf16[2048,2048]{1,0:T(8,128)(2,1)}) %all-gather.17.cloned.1.call-update) | async-done | bytes 8388624 | tf_op jit(solution)/shard_map/all_gather | solution.py:95
  183.2 7.1 convolution_add_fusion.1
  190.2 49.5 %all-gather.19.cloned.1.call-done = bf16[2048,2048]{1,0:T(8,128)(2,1)} async-done(((bf16[256,2048]{1,0:T(8,128)(2,1)}), bf16[2048,2048]{1,0:T(8,128)(2,1)}) %all-gather.19.cloned.1.call-update) | async-done | bytes 8388624 | tf_op jit(solution)/shard_map/all_gather | solution.py:142
  239.7 10.6 %convert_reduce_fusion.2 = (f32[2048]{0:T(1024)}, bf16[256,2048]{1,0:T(8,128)(2,1)S(1)}) fusion(f32[256,2048]{1,0:T(8,128)} %convolution_add_fusion.1, bf16[2048,2048]{1,0:T(8,128)(2,1)} %all-gather.19.cloned.1.call-done, bf16[1,256,2048]{2,1,0:T(8,128)(2,1)} %param.16), kind=kOutput, calls=%fused_computation.41 | convolution fusion | flops 2186278912 | bytes 12591104 | tf_op jit(solution)/shard_map/dot_general | solution.py:163
  251.3 3.7 fusion.82
  255.0 18.4 %reduce-scatter.5.cloned.1.call-done = f32[1,256,2,256]{3,1,2,0:T(8,128)} async-done(((f32[1,1024,2,256]{3,1,2,0:T(8,128)}), f32[1,256,2,256]{3,1,2,0:T(8,128)}) %reduce-scatter.5.cloned.1.call-update) | async-done | bytes 524304 | tf_op jit(solution)/shard_map/reduce_scatter | solution.py:196
  273.4 1.2 slice.153
  275.5 1.3 slice_negate_fusion
  276.8 2.2 fusion.53
  278.9 1.0 copy.91
  279.9 1.0 copy.89
  281.6 1.6 constant_dynamic-update-slice_fusion.2
  283.8 1.6 constant_dynamic-update-slice_fusion
  285.4 21.7 %reduce-scatter.7.cloned.1.call-done = f32[1,256,2,256]{1,3,2,0:T(8,128)} async-done(((f32[1,1024,2,256]{1,3,2,0:T(8,128)}), f32[1,256,2,256]{1,3,2,0:T(8,128)}) %reduce-scatter.7.cloned.1.call-update) | async-done | bytes 524304 | tf_op jit(solution)/shard_map/reduce_scatter | solution.py:197
  307.2 1.8 convert_dynamic-update-slice_fusion
  308.9 6.2 fusion.81
  315.8 2.1 convolution_convert_fusion
  318.0 8.7 fusion.76
  326.7 2.1 convolution_add_fusion
  328.9 1.1 copy-done.8
  331.6 6.6 convolution_bitcast_fusion
  338.2 10.9 %pad_maximum_fusion.1 = f32[2048,2560]{0,1:T(8,128)} fusion(f32[2048,2048]{0,1:T(8,128)S(1)} %convolution_bitcast_fusion, f32[2048,512]{0,1:T(8,128)S(1)} %convolution_bitcast_fusion.1), kind=kLoop, calls=%fused_computation.1 | loop fusion | flops 5242880 | bytes 41943040 | tf_op jit(solution)/shard_map/concatenate | solution.py:165
  350.5 2.6 fusion.69
  353.0 3.1 fusion.48
  356.1 12.3 %pad_maximum_fusion = f32[2048,3584]{0,1:T(8,128)} fusion(f32[2048,2048]{0,1:T(8,128)S(1)} %fusion.69, f32[2048,1536]{0,1:T(8,128)S(1)} %fusion.48), kind=kLoop, calls=%fused_computation | loop fusion | flops 7340032 | bytes 58720256 | tf_op jit(solution)/shard_map/concatenate | solution.py:216
  368.4 1.4 convert_reduce_fusion.3
  369.8 100.5 %all-reduce.4.cloned.1.call-done = (f32[256,2048]{1,0:T(8,128)}, f32[256,2048]{1,0:T(8,128)}) async-done(((f32[256,2048]{1,0:T(8,128)}, f32[256,2048]{1,0:T(8,128)}), (f32[256,2048]{1,0:T(8,128)}, f32[256,2048]{1,0:T(8,128)})) %all-reduce.4.cloned.1.call-update) | async-done | bytes 4194320 | tf_op jit(solution)/shard_map/psum | solution.py:225
  470.4 3.2 fusion.78
  473.8 1.6 fusion.20
  475.5 2.9 convert_reduce_fusion.1
  478.4 26.4 %all-reduce = (f32[2,768]{1,0:T(2,128)}, f32[2048]{0:T(1024)}, f32[2048]{0:T(1024)}, f32[2048]{0:T(1024)}, f32[2048]{0:T(1024)}, /*index=5*/f32[2048]{0:T(1024)}, f32[2048]{0:T(1024)}) all-reduce(f32[2,768]{1,0:T(2,128)S(1)} %convert_reduce_fusion.3, ...), channel_id=1, replica_groups=mesh['shard'=2,'ctx'=4,'tensor'=4] {'shard','ctx'}, use_global_device_ids=true, to_apply=%region_18.19 | all-reduce | flops 13824 | bytes 110592 | tf_op jit(solution)/shard_map/psum | solution.py:233
  504.8 116.2 %all-gather.21.cloned.1.call-done = f32[1024,2048]{1,0:T(8,128)} async-done(((f32[256,2048]{1,0:T(8,128)}), f32[1024,2048]{1,0:T(8,128)}) %all-gather.21.cloned.1.call-update) | async-done | bytes 8388624 | tf_op jit(solution)/shard_map/all_gather | solution.py:148
  621.0 4.4 reduce_sum.169
  625.4 1.3 fusion.25
  626.7 132.3 %reduce-scatter.11.cloned.1.call-done = f32[256,2560]{0,1:T(8,128)} async-done(((f32[2048,2560]{0,1:T(8,128)}), f32[256,2560]{0,1:T(8,128)}) %reduce-scatter.11.cloned.1.call-update) | async-done | bytes 2621456 | tf_op jit(solution)/shard_map/reduce_scatter | solution.py:164
  758.9 1.6 slice-done
  760.5 1.8 copy.96
  762.3 1.0 copy.94
  763.3 174.9 %reduce-scatter.9.cloned.1.call-done = f32[256,3584]{0,1:T(8,128)} async-done(((f32[2048,3584]{0,1:T(8,128)}), f32[256,3584]{0,1:T(8,128)}) %reduce-scatter.9.cloned.1.call-update) | async-done | bytes 3670032 | tf_op jit(solution)/shard_map/reduce_scatter | solution.py:215
  938.3 1.6 slice-done.2
  939.9 1.8 copy.95
  941.7 1.4 slice-done.3
  943.1 2.1 copy.93
  (147 shorter events, 18.0 us)
Async XLA Ops:
  7.2 3.1 copy-start.15
  7.2 4.0 copy-start.38
  7.2 5.4 copy-start
  7.2 51.4 %all-gather.9.cloned.1.call-start = ((), (), s32[]{:S(2)}) async-start(), calls=%async_computation.4 | async-start | bytes 7077888 | tf_op jit(solution)/shard_map/all_gather | solution.py:94
  10.2 78.7 %all-gather.15.cloned.1.call-start = ((), (), s32[]{:S(2)}) async-start(), calls=%async_computation.7 | async-start | bytes 2359296 | tf_op jit(solution)/shard_map/all_gather | solution.py:141
  11.2 96.6 %all-gather.13.cloned.1.call-start = ((), (), s32[]{:S(2)}) async-start(), calls=%async_computation.6 | async-start | bytes 1310720 | tf_op jit(solution)/shard_map/all_gather | solution.py:107
  12.8 61.3 %copy-start.19 = (f32[256]{0:T(256)}, f32[256]{0:T(256)S(1)}, u32[]{:S(2)}) copy-start(f32[256]{0:T(256)S(1)} %broadcast_multiply_fusion.1) | copy-start | bytes 3076
  13.3 52.1 %copy-start.25 = (f32[256]{0:T(256)}, f32[256]{0:T(256)S(1)}, u32[]{:S(2)}) copy-start(f32[256]{0:T(256)S(1)} %fusion.21) | copy-start | bytes 3076
  13.3 60.9 %copy-start.22 = (f32[256]{0:T(256)}, f32[256]{0:T(256)S(1)}, u32[]{:S(2)}) copy-start(f32[256]{0:T(256)S(1)} %fusion.65) | copy-start | bytes 3076
  65.4 8.8 copy-start.17
  65.4 8.8 copy-start.27
  65.4 8.8 copy-start.41
  78.9 2.1 copy-start.13
  78.9 1.2 copy-start.16
  80.0 3.6 copy-start.9
  81.8 44.7 %all-gather.11.cloned.1.call-start = ((), (), s32[]{:S(2)}) async-start(), calls=%async_computation.5 | async-start | bytes 1310720 | tf_op jit(solution)/shard_map/all_gather | solution.py:108
  83.5 99.6 %all-gather.17.cloned.1.call-start = ((), (), s32[]{:S(2)}) async-start(), calls=%async_computation.8 | async-start | bytes 9437184 | tf_op jit(solution)/shard_map/all_gather | solution.py:95
  84.7 2.9 copy-start.37
  84.8 155.0 %all-gather.19.cloned.1.call-start = ((), (), s32[]{:S(2)}) async-start(), calls=%async_computation.9 | async-start | bytes 9437184 | tf_op jit(solution)/shard_map/all_gather | solution.py:142
  87.6 185.9 %reduce-scatter.5.cloned.1.call-start = ((), (), s32[]{:S(2)}) async-start(), calls=%async_computation.10 | async-start | bytes 2621440 | tf_op jit(solution)/shard_map/reduce_scatter | solution.py:196
  88.9 3.5 copy-start.7
  91.1 1.3 copy-start.4
  109.8 0.6 copy-start.33
  110.4 0.6 copy-start.35
  128.2 1.5 copy-start.12
  128.3 1.5 copy-start.14
  128.8 1.0 copy-start.3
  131.7 175.4 %reduce-scatter.7.cloned.1.call-start = ((), (), s32[]{:S(2)}) async-start(), calls=%async_computation.11 | async-start | bytes 2621440 | tf_op jit(solution)/shard_map/reduce_scatter | solution.py:197
  134.4 0.8 copy-start.6
  139.7 43.4 %copy-start.18 = (f32[2048]{0:T(1024)S(1)}, f32[2048]{0:T(1024)}, u32[]{:S(2)}) copy-start(f32[2048]{0:T(1024)} %param.28) | copy-start | bytes 24580
  139.7 43.4 %copy-start.20 = (f32[256]{0:T(256)S(1)}, f32[256]{0:T(256)}, u32[]{:S(2)}) copy-start(f32[256]{0:T(256)} %copy-done.19) | copy-start | bytes 3076
  139.7 43.4 %copy-start.23 = (f32[256]{0:T(256)S(1)}, f32[256]{0:T(256)}, u32[]{:S(2)}) copy-start(f32[256]{0:T(256)} %copy-done.22) | copy-start | bytes 3076
  139.7 43.4 %copy-start.29 = (f32[2048]{0:T(1024)S(1)}, f32[2048]{0:T(1024)}, u32[]{:S(2)}) copy-start(f32[2048]{0:T(1024)} %param.29) | copy-start | bytes 24580
  139.7 43.4 %copy-start.40 = (f32[2048]{0:T(1024)S(1)}, f32[2048]{0:T(1024)}, u32[]{:S(2)}) copy-start(f32[2048]{0:T(1024)} %param.23) | copy-start | bytes 24580
  141.7 328.6 %all-reduce.4.cloned.1.call-start = ((), (), s32[]{:S(2)}) async-start(), calls=%async_computation.15 | async-start | bytes 8388608 | tf_op jit(solution)/shard_map/psum | solution.py:225
  239.7 11.6 %copy-start.39 = (bf16[2048,2048]{1,0:T(8,128)(2,1)S(1)}, bf16[2048,2048]{1,0:T(8,128)(2,1)}, u32[]{:S(2)}) copy-start(bf16[2048,2048]{1,0:T(8,128)(2,1)} %all-gather.17.cloned.1.call-done) | copy-start | bytes 25165828
  250.3 1.0 copy-start.10
  315.1 0.7 copy-start.34
  315.1 0.7 copy-start.36
  315.2 305.8 %all-gather.21.cloned.1.call-start = ((), (), s32[]{:S(2)}) async-start(), calls=%async_computation.14 | async-start | bytes 10485760 | tf_op jit(solution)/shard_map/all_gather | solution.py:148
  315.8 2.1 copy-start.42
  317.9 8.7 copy-start.5
  328.8 1.2 copy-start.8
  328.8 430.1 %reduce-scatter.11.cloned.1.call-start = ((), (), s32[]{:S(2)}) async-start(), calls=%async_computation.13 | async-start | bytes 23592960 | tf_op jit(solution)/shard_map/reduce_scatter | solution.py:164
  330.0 1.6 copy-start.43
  349.2 1.3 copy-start.11
  349.2 1.3 copy-start.21
  349.2 1.3 copy-start.24
  349.2 1.3 copy-start.30
  349.2 3.8 copy-start.28
  349.2 589.0 %reduce-scatter.9.cloned.1.call-start = ((), (), s32[]{:S(2)}) async-start(), calls=%async_computation.12 | async-start | bytes 33030144 | tf_op jit(solution)/shard_map/reduce_scatter | solution.py:215
  470.3 3.2 copy-start.26
  470.3 3.3 copy-start.1
  470.3 3.5 copy-start.2
  475.5 2.9 copy-start.32
  621.0 4.4 copy-start.31
  758.9 1.6 slice-start
  760.5 1.8 slice-start.1
  938.3 1.6 slice-start.2
  941.7 1.4 slice-start.3
Sparse Core Ops, SparseCore 0:
  10.5 48.1 all-gather.8
  61.1 27.7 all-gather.14
  91.1 16.6 all-gather.12
  109.8 16.6 all-gather.10
  128.8 54.2 all-gather.16
  185.4 54.2 all-gather.18
  242.3 31.1 reduce-scatter.4
  276.0 31.1 reduce-scatter.6
  315.3 155.0 all-reduce.3
  472.3 148.5 all-gather.20
  624.6 134.3 reduce-scatter.10
  762.4 175.8 reduce-scatter.8
